TPU v7x, 32 devices: a whole 2x2x4 slice. The times are simulated.
32 devices in a mesh: gauss: 4 (over y, core), tile: 8 (over z, x).
Axes of the slice: x: 2, y: 2, z: 4, core: 2. Of those that a mesh axis runs over, the one named last changes fastest.
Arguments:
- params: float32 [59, 16384], P(None, ('gauss', 'tile')), as said below
- moment_one: float32 [59, 16384], P(None, ('gauss', 'tile')), may hold values from -1.8 to 1.8
- moment_two: float32 [59, 16384], P(None, ('gauss', 'tile')), may hold values from 1e-06 to 0.01
- camera: float32 [3, 11], replicated, as said below
- target: float32 [3, 3, 32, 256], P(None, None, ('gauss', 'tile')), may hold values from 0 to 1
- tile_ids: int32 [3, 32], P(None, ('gauss', 'tile')), may hold values from 0 to 31, as said below
- splat_lists: int32 [3, 32, 256], P(None, ('gauss', 'tile')), may hold values from 0 to 16383, as said below
- counts: int32 [3, 32], P(None, ('gauss', 'tile')), may hold values from 32 to 256, as said below
Outputs:
- new_params: float32 [59, 16384], P(None, ('gauss', 'tile'))
- new_first: float32 [59, 16384], P(None, ('gauss', 'tile'))
- new_second: float32 [59, 16384], P(None, ('gauss', 'tile'))
- rendered: float32 [3, 3, 32, 256], P(None, None, ('gauss', 'tile'))
- view_losses: float32 [3], replicated
Inputs may be any that keep to these rules, and one draw needn't show every extreme that they name: `splat_lists`: entries of slot q lie in [b * 4096, (b + 1) * 4096) with b = q // 8; entries at or past the slot's count are padding. `counts`: every view has a slot whose count is 256. `tile_ids`: in each view the slots q with q // 8 = b hold each tile of b * 8 to (b + 1) * 8 - 1 once. `params`: row 6 lies in [0.5, 1.5]. `camera`: entries 8 to 10 of each row form a unit vector.
All inputs are finite; a program needn't handle non-finite values.
Results may differ from a plain program's by a relative error of at most 0.0003.
Values sent between devices are 32-bit elements; how exact they have to be, the bound alone decides.
A program may use at most 64 MiB of HBM per device.

v0:
```python
import jax
import jax.numpy as jnp
from jax import lax
from jax.sharding import PartitionSpec as P

VIEWS = 3
TILES_WIDE = 4


band_zero = 0.28209479177387814
band_one = 0.4886025119029199
band_two = (
    1.0925484305920792,
    -1.0925484305920792,
    0.31539156525252005,
    -1.0925484305920792,
    0.5462742152960396,
)
band_three = (
    -0.5900435899266435,
    2.890611442640554,
    -0.4570457994644658,
    0.3731763325901154,
    -0.4570457994644658,
    1.445305721320277,
    -0.5900435899266435,
)
learning_rates = (
    (0.00016,) * 3 + (0.005,) * 3 + (0.001,) * 4 + (0.05,) + (0.0025,) * 3 + (0.000125,) * 45
)
highest = lax.Precision.HIGHEST


def harmonics(facing):
    facing_x, facing_y, facing_z = (facing[0], facing[1], facing[2])
    square_x, square_y, square_z = (facing_x * facing_x, facing_y * facing_y, facing_z * facing_z)
    return jnp.stack(
        [
            band_zero + 0.0 * facing_x,
            -band_one * facing_y,
            band_one * facing_z,
            -band_one * facing_x,
            band_two[0] * facing_x * facing_y,
            band_two[1] * facing_y * facing_z,
            band_two[2] * (2.0 * square_z - square_x - square_y),
            band_two[3] * facing_x * facing_z,
            band_two[4] * (square_x - square_y),
            band_three[0] * facing_y * (3.0 * square_x - square_y),
            band_three[1] * facing_x * facing_y * facing_z,
            band_three[2] * facing_y * (4.0 * square_z - square_x - square_y),
            band_three[3] * facing_z * (2.0 * square_z - 3.0 * square_x - 3.0 * square_y),
            band_three[4] * facing_x * (4.0 * square_z - square_x - square_y),
            band_three[5] * facing_z * (square_x - square_y),
            band_three[6] * facing_x * (square_x - 3.0 * square_y),
        ]
    )


def project(params, camera):
    quaternion = params[6:10]
    quat_norm = jnp.sqrt(jnp.sum(quaternion * quaternion, axis=0))
    quat_w, quat_x, quat_y, quat_z = [quaternion[component] / quat_norm for component in range(4)]
    rotation = jnp.stack(
        [
            1.0 - 2.0 * (quat_y * quat_y + quat_z * quat_z),
            2.0 * (quat_x * quat_y - quat_w * quat_z),
            2.0 * (quat_x * quat_z + quat_w * quat_y),
            2.0 * (quat_x * quat_y + quat_w * quat_z),
            1.0 - 2.0 * (quat_x * quat_x + quat_z * quat_z),
            2.0 * (quat_y * quat_z - quat_w * quat_x),
            2.0 * (quat_x * quat_z - quat_w * quat_y),
            2.0 * (quat_y * quat_z + quat_w * quat_x),
            1.0 - 2.0 * (quat_x * quat_x + quat_y * quat_y),
        ]
    ).reshape(3, 3, -1)
    stretched = rotation * jnp.exp(params[3:6])[None, :, :]
    affine = camera[0:6].reshape(2, 3)
    screen_axes = jnp.einsum("ki,ijn->kjn", affine, stretched, precision=highest)
    cov_a = jnp.sum(screen_axes[0] * screen_axes[0], axis=0) + 0.3
    cov_b = jnp.sum(screen_axes[0] * screen_axes[1], axis=0)
    cov_c = jnp.sum(screen_axes[1] * screen_axes[1], axis=0) + 0.3
    determinant = cov_a * cov_c - cov_b * cov_b
    centre_px = (
        jnp.einsum("ki,in->kn", affine, params[0:3], precision=highest) + camera[6:8][:, None]
    )
    opacity = jax.nn.sigmoid(params[10])
    coeffs = params[11:59].reshape(16, 3, -1)
    colour = jnp.maximum(
        jnp.einsum("i,ikn->kn", harmonics(camera[8:11]), coeffs, precision=highest) + 0.5, 0.0
    )
    return jnp.concatenate(
        [
            centre_px,
            jnp.stack([cov_c / determinant, -cov_b / determinant, cov_a / determinant, opacity]),
            colour,
        ],
        axis=0,
    )


def shade(splat_attrs, live_count, tile_id):
    pixel_index = jnp.arange(256, dtype=jnp.int32)
    pixel_x = (tile_id % TILES_WIDE * 16 + pixel_index % 16).astype(jnp.float32) + 0.5
    pixel_y = (tile_id // TILES_WIDE * 16 + pixel_index // 16).astype(jnp.float32) + 0.5
    offset_x = pixel_x[:, None] - splat_attrs[0][None, :]
    offset_y = pixel_y[:, None] - splat_attrs[1][None, :]
    exponent = (
        -0.5 * (splat_attrs[2] * offset_x * offset_x + splat_attrs[4] * offset_y * offset_y)
        - splat_attrs[3] * offset_x * offset_y
    )
    live_slots = jnp.arange(splat_attrs.shape[1], dtype=jnp.int32) < live_count
    coverage = jnp.where(
        live_slots[None, :], jnp.minimum(0.99, splat_attrs[5] * jnp.exp(exponent)), 0.0
    )
    log_keep = jnp.log(1.0 - coverage)
    before = jnp.concatenate(
        [jnp.zeros_like(log_keep[:, :1]), jnp.cumsum(log_keep[:, :-1], axis=1)], axis=1
    )
    weights = coverage * jnp.exp(before)
    return jnp.einsum("pj,kj->kp", weights, splat_attrs[6:9], precision=highest)


def render_view(band_attrs, local_ids, live_counts, view_tiles, view_target, grad_scale):

    def one_tile(splat_ids, live_count, tile_id, target_tile):
        splat_attrs = jnp.take(band_attrs, splat_ids, axis=1)
        colours, tile_back = jax.vjp(lambda values: shade(values, live_count, tile_id), splat_attrs)
        residual = colours - target_tile
        (attr_grad,) = tile_back(residual * grad_scale)
        return (colours, jnp.sum(residual * residual), attr_grad)

    colours, squared, attr_grads = jax.vmap(one_tile)(
        local_ids, live_counts, view_tiles, jnp.transpose(view_target, (1, 0, 2))
    )
    flat_grad = jnp.transpose(attr_grads, (1, 0, 2)).reshape(9, -1)
    band_grad = jnp.zeros_like(band_attrs).at[:, local_ids.reshape(-1)].add(flat_grad)
    return (jnp.transpose(colours, (1, 0, 2)), jnp.sum(squared), band_grad)


def shards(params, moment_one, moment_two, camera, target, tile_ids, splat_lists, counts):
    grad_scale = 1.0 / (VIEWS * 256)
    band_size = params.shape[1] * lax.axis_size("tile")
    local_ids = splat_lists - lax.axis_index("gauss") * band_size
    images_all = []
    squared_all = []
    gradient = jnp.zeros_like(params)
    for view_index in range(VIEWS):
        attrs_own, pullback = jax.vjp(lambda values: project(values, camera[view_index]), params)
        band_attrs = lax.all_gather(attrs_own, "tile", axis=1, tiled=True)
        colours, squared, band_grad = render_view(
            band_attrs,
            local_ids[view_index],
            counts[view_index],
            tile_ids[view_index],
            target[view_index],
            grad_scale,
        )
        own_grad = lax.psum_scatter(band_grad, "tile", scatter_dimension=1, tiled=True)
        gradient = gradient + pullback(own_grad)[0]
        images_all.append(colours)
        squared_all.append(squared)
    totals = lax.psum(jnp.stack(squared_all), ("gauss", "tile"))
    tiles_all = counts.shape[1] * lax.axis_size("gauss") * lax.axis_size("tile")
    losses = 0.5 * totals / (3 * 256 * tiles_all)
    rates = jnp.array(learning_rates, dtype=jnp.float32)[:, None]
    first = 0.9 * moment_one + 0.1 * gradient
    second = 0.999 * moment_two + 0.001 * gradient * gradient
    updated = params - rates * first / (jnp.sqrt(second) + 1e-15)
    return (updated, first, second, jnp.stack(images_all), losses)


def solution(mesh):
    return jax.shard_map(
        shards,
        mesh=mesh,
        in_specs=(
            P(None, ("gauss", "tile")),
            P(None, ("gauss", "tile")),
            P(None, ("gauss", "tile")),
            P(),
            P(None, None, ("gauss", "tile"), None),
            P(None, ("gauss", "tile")),
            P(None, ("gauss", "tile"), None),
            P(None, ("gauss", "tile")),
        ),
        out_specs=(
            P(None, ("gauss", "tile")),
            P(None, ("gauss", "tile")),
            P(None, ("gauss", "tile")),
            P(None, None, ("gauss", "tile"), None),
            P(),
        ),
        check_vma=False,
    )
```

profile of v0, /device:TPU:0, one launch (start us, length us, event | category | flops | bytes accessed | tf_op | source)
XLA Modules:
  0.0 291.3 jit_solution(3546840454794751938)
XLA Ops:
  7.2 0.8 slice_reduce_fusion.20
  8.0 0.9 slice_bitcast_fusion.22
  8.9 0.8 multiply_reduce_fusion.6
  9.7 0.7 slice_exponential_fusion
  10.4 0.9 slice.350
  11.3 1.7 fusion.418
  21.7 0.7 broadcast_subtract_fusion
  22.4 1.4 fusion.420
  26.3 0.9 multiply_subtract_fusion.6
  27.3 0.8 add_multiply_fusion
  35.4 0.8 convolution_add_fusion.2
  36.4 32.6 %all_gather.9 = f32[9,4096]{1,0:T(8,128)S(1)} all-gather(f32[9,512]{1,0:T(8,128)S(1)} %concatenate.18), channel_id=1, replica_groups=mesh['gauss'=4,'tile'=8] {'tile'}, dimensions={1}, use_global_device_ids=true | all-gather | bytes 165888 | tf_op jit(solution)/shard_map/all_gather | solution.py:149
  69.0 0.6 copy.66
  69.7 0.7 gather_fusion
  71.0 0.6 fusion.419
  73.0 1.2 fusion.43
  75.2 1.0 multiply_reduce_fusion.18
  77.0 2.3 fusion.148
  80.2 0.7 fusion.29
  81.0 1.9 scatter_custom_fusion
  83.0 1.3 copy.78
  103.9 30.9 %all_gather.10 = f32[9,4096]{1,0:T(8,128)S(1)} all-gather(f32[9,512]{1,0:T(8,128)S(1)} %concatenate.20), channel_id=1, replica_groups=mesh['gauss'=4,'tile'=8] {'tile'}, dimensions={1}, use_global_device_ids=true | all-gather | bytes 165888 | tf_op jit(solution)/shard_map/all_gather | solution.py:149
  134.9 0.6 copy.82
  135.5 0.7 gather_fusion.1
  136.9 0.6 fusion.197
  138.2 1.1 fusion.55
  140.5 1.0 multiply_reduce_fusion.17
  142.3 2.3 fusion.146
  145.1 0.7 fusion.23
  146.3 1.9 scatter_custom_fusion.1
  148.2 1.3 copy.94
  169.6 31.0 %all_gather.11 = f32[9,4096]{1,0:T(8,128)S(1)} all-gather(f32[9,512]{1,0:T(8,128)S(1)} %concatenate.22), channel_id=1, replica_groups=mesh['gauss'=4,'tile'=8] {'tile'}, dimensions={1}, use_global_device_ids=true | all-gather | bytes 165888 | tf_op jit(solution)/shard_map/all_gather | solution.py:149
  201.3 0.7 gather_fusion.2
  202.7 0.7 fusion.196
  204.0 1.1 fusion.67
  205.2 0.6 iota_compare_fusion
  206.3 1.0 multiply_reduce_fusion.16
  208.1 2.3 fusion.144
  210.9 0.7 fusion.17
  212.1 1.9 scatter_custom_fusion.2
  214.0 1.3 copy.110
  215.4 2.0 pad_maximum_fusion.1
  217.4 39.6 %psum.7 = f32[3]{0:T(128)S(1)} all-reduce(f32[3]{0:T(128)S(1)} %pad_maximum_fusion.1), channel_id=1, replica_groups=mesh['gauss'=4,'tile'=8] {'gauss','tile'}, use_global_device_ids=true, to_apply=%region_52.54 | all-reduce | flops 3 | bytes 24 | tf_op jit(solution)/shard_map/psum | solution.py:162
  258.1 20.5 %reduce-scatter.8.cloned.1.call-done = f32[9,512]{1,0:T(8,128)} async-done(((f32[9,4096]{1,0:T(8,128)}), f32[9,512]{1,0:T(8,128)}) %reduce-scatter.8.cloned.1.call-update) | async-done | bytes 18448 | tf_op jit(solution)/shard_map/reduce_scatter | solution.py:158
  278.6 1.0 slice_multiply_fusion.23
  281.0 0.8 slice_multiply_fusion
  281.9 0.8 slice_multiply_fusion.1
  283.9 0.8 divide_subtract_fusion
  (219 shorter events, 19.5 us)
Async XLA Ops:
  7.2 250.9 %reduce-scatter.4.cloned.1.call-start = ((), (), s32[]{:S(2)}) async-start(), calls=%async_computation.3 | async-start | bytes 294912 | tf_op jit(solution)/shard_map/reduce_scatter | solution.py:158
  35.1 36.0 %copy-start.9 = (s32[3,1]{0,1:T(1,128)S(1)}, s32[3,1]{0,1:T(1,128)}, u32[]{:S(2)}) copy-start(s32[3,1]{0,1:T(1,128)} %param.18) | copy-start | bytes 40
  69.0 4.0 %copy-start.1 = (pred[2,128]{0,1:T(32,128)(4,1)S(1)}, pred[2,128]{0,1:T(32,128)(4,1)}, u32[]{:S(2)}) copy-start(pred[2,128]{0,1:T(32,128)(4,1)} %constant.272.clone.1) | copy-start | bytes 772
  69.0 5.8 %copy-start.4 = (f32[3,3,1,256]{3,2,1,0:T(1,128)S(1)}, f32[3,3,1,256]{3,2,1,0:T(1,128)}, u32[]{:S(2)}) copy-start(f32[3,3,1,256]{3,2,1,0:T(1,128)} %param.15) | copy-start | bytes 27652
  75.2 4.5 %copy-start.8 = (pred[256]{0:T(512)(128)(4,1)S(1)}, pred[256]{0:T(512)(128)(4,1)}, u32[]{:S(2)}) copy-start(pred[256]{0:T(512)(128)(4,1)} %constant.275.clone.1) | copy-start | bytes 772
  81.0 22.6 %copy-start = (f32[59,512]{1,0:T(8,128)S(1)}, f32[59,512]{1,0:T(8,128)}, u32[]{:S(2)}) copy-start(f32[59,512]{1,0:T(8,128)} %param.11) | copy-start | bytes 362500
  84.3 173.8 %reduce-scatter.6.cloned.1.call-start = ((), (), s32[]{:S(2)}) async-start(), calls=%async_computation.4 | async-start | bytes 294912 | tf_op jit(solution)/shard_map/reduce_scatter | solution.py:158
  149.6 129.1 %reduce-scatter.8.cloned.1.call-start = ((), (), s32[]{:S(2)}) async-start(), calls=%async_computation.5 | async-start | bytes 294912 | tf_op jit(solution)/shard_map/reduce_scatter | solution.py:158
  215.3 68.5 %copy-start.2 = (f32[59,512]{1,0:T(8,128)S(1)}, f32[59,512]{1,0:T(8,128)}, u32[]{:S(2)}) copy-start(f32[59,512]{1,0:T(8,128)} %param.12) | copy-start | bytes 362500
  215.3 68.5 %copy-start.3 = (f32[59,512]{1,0:T(8,128)S(1)}, f32[59,512]{1,0:T(8,128)}, u32[]{:S(2)}) copy-start(f32[59,512]{1,0:T(8,128)} %param.13) | copy-start | bytes 362500
  215.3 68.5 %copy-start.10 = (f32[59]{0:T(128)S(1)}, f32[59]{0:T(128)}, u32[]{:S(2)}) copy-start(f32[59]{0:T(128)} %constant.281.clone) | copy-start | bytes 712
  258.1 24.8 %copy-start.5 = (f32[9,512]{1,0:T(8,128)S(1)}, f32[9,512]{1,0:T(8,128)}, u32[]{:S(2)}) copy-start(f32[9,512]{1,0:T(8,128)} %reduce-scatter.4.cloned.1.call-done) | copy-start | bytes 55300
  258.1 25.4 %copy-start.6 = (f32[9,512]{1,0:T(8,128)S(1)}, f32[9,512]{1,0:T(8,128)}, u32[]{:S(2)}) copy-start(f32[9,512]{1,0:T(8,128)} %reduce-scatter.6.cloned.1.call-done) | copy-start | bytes 55300
  278.6 4.6 %copy-start.7 = (f32[9,512]{1,0:T(8,128)S(1)}, f32[9,512]{1,0:T(8,128)}, u32[]{:S(2)}) copy-start(f32[9,512]{1,0:T(8,128)} %reduce-scatter.8.cloned.1.call-done) | copy-start | bytes 55300
Sparse Core Ops, SparseCore 0:
  84.4 63.1 reduce-scatter.3
  150.9 61.7 reduce-scatter.5
  216.1 62.5 reduce-scatter.7
where the time goes:
time: 293 us; the launch traced here: 291 us
  blocking collectives  134 us (46%)
  between operations  70.3 us (24%)
  other arithmetic  36.2 us (12%)
  local copies, waits for them, and re-layouts  21.5 us (7%)
  waiting for transfers between devices  20.6 us (7%)
  matrix products  8.56 us (3%)
    all_gather x3, blocking collectives, shards(): band_attrs = lax.all_gather(attrs_own, 'tile', axis=1, tiled=True)  94.5 us
    psum x1, blocking collectives, shards(): totals = lax.psum(jnp.stack(squared_all), ('gauss', 'tile'))  39.6 us
    reduce_scatter x3, waiting for transfers between devices, shards(): lax.psum_scatter(band_grad, 'tile', scatter_dimension=1, tiled=True)  20.5 us
    another operation x15, other arithmetic  10.7 us
  transfers between devices with their start and end apart: 3, of which 1 were waited for; matrix products, arithmetic and copies ran while one was open for 12% of the time, Pallas kernels for 0%

commit v1 on v0

v1 whole, which is shorter than its diff:
```python
import functools

import jax
import jax.numpy as jnp
from jax import lax
from jax.experimental import pallas as pl
from jax.experimental.pallas import tpu as pltpu
from jax.sharding import PartitionSpec as P

MESH = pl.DeviceIdType.MESH
VIEWS = 3
TILES_WIDE = 4


band_zero = 0.28209479177387814
band_one = 0.4886025119029199
band_two = (
    1.0925484305920792,
    -1.0925484305920792,
    0.31539156525252005,
    -1.0925484305920792,
    0.5462742152960396,
)
band_three = (
    -0.5900435899266435,
    2.890611442640554,
    -0.4570457994644658,
    0.3731763325901154,
    -0.4570457994644658,
    1.445305721320277,
    -0.5900435899266435,
)
learning_rates = (
    (0.00016,) * 3 + (0.005,) * 3 + (0.001,) * 4 + (0.05,) + (0.0025,) * 3 + (0.000125,) * 45
)
highest = lax.Precision.HIGHEST


def split(value, parts):
    pieces = []
    rest = value
    for _ in range(parts - 1):
        piece = rest.astype(jnp.bfloat16)
        pieces.append(piece)
        rest = rest - piece.astype(jnp.float32)
    pieces.append(rest.astype(jnp.bfloat16))
    return pieces


def dot(left, right, dims, precision=None):
    return lax.dot_general(
        left, right, (dims, ((), ())), precision=precision, preferred_element_type=jnp.float32
    )


def harmonics(x, y, z):
    xx, yy, zz = x * x, y * y, z * z
    return [
        band_zero + 0.0 * x,
        -band_one * y,
        band_one * z,
        -band_one * x,
        band_two[0] * x * y,
        band_two[1] * y * z,
        band_two[2] * (2.0 * zz - xx - yy),
        band_two[3] * x * z,
        band_two[4] * (xx - yy),
        band_three[0] * y * (3.0 * xx - yy),
        band_three[1] * x * y * z,
        band_three[2] * y * (4.0 * zz - xx - yy),
        band_three[3] * z * (2.0 * zz - 3.0 * xx - 3.0 * yy),
        band_three[4] * x * (4.0 * zz - xx - yy),
        band_three[5] * z * (xx - yy),
        band_three[6] * x * (xx - 3.0 * yy),
    ]


def iota(shape, dim):
    return lax.broadcasted_iota(jnp.int32, shape, dim)


def basis(camera, n_params):
    rows = 8 * VIEWS
    row, lane = iota((rows, n_params), 0), iota((rows, n_params), 1)
    quantity, view = row % 8, row // 8

    def entry(index):
        value = jnp.full((rows, n_params), camera[VIEWS - 1, index], jnp.float32)
        for v in range(VIEWS - 1):
            value = jnp.where(view == v, camera[v, index], value)
        return value

    out = jnp.zeros((rows, n_params), jnp.float32)
    for k in range(2):
        for i in range(3):
            out = jnp.where((quantity == k) & (lane == i), entry(3 * k + i), out)
    term, channel = (lane - 11) // 3, (lane - 11) % 3
    own = (lane >= 11) & (channel == quantity - 5)
    for i, value in enumerate(harmonics(entry(8), entry(9), entry(10))):
        out = jnp.where(own & (term == i), value, out)
    return out


def kernel(
    n_tile,
    n_gauss,
    params_ref,
    camera,
    target_ref,
    tile_ids,
    lists_ref,
    counts,
    grad_ref,
    image_ref,
    loss_ref,
    attrs,
    parts,
    totals,
    upper,
    lower,
    alpha_ref,
    raw_ref,
    log_ref,
    send_a,
    recv_a,
    send_g,
    recv_g,
    send_l,
    recv_l,
):
    me, mg = lax.axis_index("tile"), lax.axis_index("gauss")
    n_params, own = params_ref.shape
    blocks = own // 128
    size = lists_ref.shape[2]
    rows = 8 * VIEWS
    id_row = blocks * rows + 8
    scale = 1.0 / (VIEWS * 256)

    barrier = pltpu.get_barrier_semaphore()
    for d in range(1, n_tile):
        pl.semaphore_signal(
            barrier, inc=1, device_id={"tile": lax.rem(me + d, n_tile)}, device_id_type=MESH
        )
    for d in range(1, n_gauss):
        pl.semaphore_signal(
            barrier, inc=1, device_id={"gauss": lax.rem(mg + d, n_gauss)}, device_id_type=MESH
        )

    table = basis(camera, n_params)
    view_of = iota((VIEWS, own), 0)

    def entry(index):
        value = jnp.full((VIEWS, own), camera[VIEWS - 1, index], jnp.float32)
        for v in range(VIEWS - 1):
            value = jnp.where(view_of == v, camera[v, index], value)
        return value

    affine = [[entry(3 * k + i) for i in range(3)] for k in range(2)]
    params = params_ref[...]
    quat = [params_ref[6 + i : 7 + i, :] for i in range(4)]
    norm = jnp.sqrt(quat[0] * quat[0] + quat[1] * quat[1] + quat[2] * quat[2] + quat[3] * quat[3])
    w, x, y, z = [part / norm for part in quat]
    rot = [
        [1.0 - 2.0 * (y * y + z * z), 2.0 * (x * y - w * z), 2.0 * (x * z + w * y)],
        [2.0 * (x * y + w * z), 1.0 - 2.0 * (x * x + z * z), 2.0 * (y * z - w * x)],
        [2.0 * (x * z - w * y), 2.0 * (y * z + w * x), 1.0 - 2.0 * (x * x + y * y)],
    ]
    stretch = [jnp.exp(params_ref[3 + j : 4 + j, :]) for j in range(3)]
    axes = [
        [sum(affine[k][i] * (rot[i][j] * stretch[j]) for i in range(3)) for j in range(3)]
        for k in range(2)
    ]
    cov_a = sum(axes[0][j] * axes[0][j] for j in range(3)) + 0.3
    cov_b = sum(axes[0][j] * axes[1][j] for j in range(3))
    cov_c = sum(axes[1][j] * axes[1][j] for j in range(3)) + 0.3
    determinant = cov_a * cov_c - cov_b * cov_b
    conic = [cov_c / determinant, -cov_b / determinant, cov_a / determinant]
    opacity = jax.nn.sigmoid(params_ref[10:11, :])

    linear = dot(table, params, ((1,), (0,)), highest)
    quantity = iota((8, own), 0)
    linear_views = []
    for v in range(VIEWS):
        shift = jnp.where(
            quantity == 0, camera[v, 6], jnp.where(quantity == 1, camera[v, 7], 0.5)
        )
        value = linear[8 * v : 8 * v + 8] + shift
        linear_views.append(value)
        value = jnp.where(quantity >= 5, jnp.maximum(value, 0.0), value)
        for q in range(3):
            value = jnp.where(quantity == 2 + q, conic[q][v : v + 1], value)
        for b in range(blocks):
            attrs[me, b * rows + 8 * v : b * rows + 8 * v + 8, :] = value[
                :, 128 * b : 128 * b + 128
            ]
    base = mg * (own * n_tile)
    spare = attrs.shape[1] - blocks * rows
    attrs[me, blocks * rows :, :] = jnp.zeros((spare, 128), jnp.float32)
    for b in range(blocks):
        attrs[me, blocks * rows + b : blocks * rows + b + 1, :] = opacity[
            :, 128 * b : 128 * b + 128
        ]
    for v in range(VIEWS):
        ids = (lists_ref[v] - base).astype(jnp.float32)
        for h in range(size // 128):
            place = id_row + v * (size // 128) + h
            attrs[me, place : place + 1, :] = ids[:, 128 * h : 128 * h + 128]

    pl.semaphore_wait(barrier, n_tile + n_gauss - 2)
    sends = []
    for d in range(1, n_tile):
        copy = pltpu.make_async_remote_copy(
            src_ref=attrs.at[me],
            dst_ref=attrs.at[me],
            send_sem=send_a.at[d],
            recv_sem=recv_a.at[d],
            device_id={"tile": lax.rem(me + d, n_tile)},
            device_id_type=MESH,
        )
        copy.start()
        sends.append(copy)

    before_j = (iota((size, size), 0) < iota((size, size), 1)).astype(jnp.float32)
    after_j = (iota((size, size), 0) > iota((size, size), 1)).astype(jnp.float32)
    for c in range(2):
        upper[c * size : (c + 1) * size, :] = before_j.astype(jnp.bfloat16)
        lower[c * size : (c + 1) * size, :] = after_j.astype(jnp.bfloat16)
    parts[me, rows + 2 * VIEWS : rows + 8, :] = jnp.zeros((8 - 2 * VIEWS, size), jnp.float32)
    for copy in sends:
        copy.wait()

    grad_sends = []
    pixel_col = iota((16, size), 0).astype(jnp.float32) + 0.5
    lane = iota((1, size), 1)
    low_of = iota((128, size), 0)
    op_row = iota((8 * n_tile, size), 0)
    op_high = jnp.where(op_row % 8 < blocks, op_row // 8 * blocks + op_row % 8, -1)
    for v in range(VIEWS):
        ids = lists_ref[v] - base
        high, low = ids // 128, ids % 128
        onehot = (low_of == low).astype(jnp.float32).astype(jnp.bfloat16)
        tiles = [
            attrs[s, b * rows + 8 * v : b * rows + 8 * v + 8, :]
            for s in range(n_tile)
            for b in range(blocks)
        ] + [attrs[s, blocks * rows : blocks * rows + 8, :] for s in range(n_tile)]
        pieces = jnp.concatenate(split(jnp.concatenate(tiles, axis=0), 3), axis=1)
        picked = dot(pieces, jnp.concatenate([onehot] * 3, axis=0), ((1,), (0,)))
        splat = jnp.zeros((8, size), jnp.float32)
        for h in range(n_tile * blocks):
            splat = jnp.where(high == h, picked[8 * h : 8 * h + 8], splat)
        opac = jnp.sum(
            jnp.where(op_high == high, picked[8 * n_tile * blocks :], 0.0), axis=0, keepdims=True
        )
        mean_x, mean_y = splat[0:1], splat[1:2]
        con0, con1, con2 = splat[2:3], splat[3:4], splat[4:5]
        tile = tile_ids[v]
        corner_x = (tile % TILES_WIDE * 16).astype(jnp.float32)
        corner_y = (tile // TILES_WIDE * 16).astype(jnp.float32)
        live = lane < counts[v]
        dx = pixel_col + corner_x - mean_x
        part_x = -0.5 * con0 * dx * dx
        opac_live = jnp.where(live, opac, 0.0)
        dys = []
        for r in range(16):
            dy = (corner_y + (r + 0.5)) - mean_y
            dys.append(dy)
            exponent = part_x - 0.5 * con2 * dy * dy - (con1 * dy) * dx
            raw = jnp.where(live, opac_live * jnp.exp(exponent), 0.0)
            cover = jnp.minimum(0.99, raw)
            log_keep = jnp.log(1.0 - cover)
            alpha_ref[16 * r : 16 * r + 16, :] = cover
            raw_ref[16 * r : 16 * r + 16, :] = jnp.where(
                raw < 0.99, raw, jnp.where(raw == 0.99, 0.5 * raw, 0.0)
            )
            for c, piece in enumerate(split(log_keep, 2)):
                log_ref[16 * r : 16 * r + 16, c * size : (c + 1) * size] = piece
        trans = jnp.exp(dot(log_ref[...], upper[...], ((1,), (0,))))
        cover = alpha_ref[...]
        weights = cover * trans
        w_split = split(weights, 2)
        colour = jnp.where(iota((8, size), 0) < 3, jnp.concatenate([splat[5:8], splat[0:5]], axis=0), 0.0)
        c_split = jnp.concatenate([p.astype(jnp.float32) for p in split(colour, 3)], axis=0)
        c_split = jnp.concatenate([c_split, jnp.zeros_like(colour)], axis=0).astype(jnp.bfloat16)
        image = dot(c_split, w_split[0], ((1,), (1,))) + dot(c_split, w_split[1], ((1,), (1,)))
        image = image[0:8] + image[8:16] + image[16:24]
        residuals = []
        square = jnp.zeros((1, 256), jnp.float32)
        for k in range(3):
            image_ref[v, k] = image[k : k + 1]
            residual = image[k : k + 1] - target_ref[v, k]
            square = square + residual * residual
            residuals.append(residual * scale)
        resid = jnp.concatenate(residuals + [jnp.zeros((5, 256), jnp.float32)], axis=0)
        slope = dot(resid, colour, ((0,), (0,)), highest)
        later = dot(
            jnp.concatenate(split(weights * slope, 2), axis=1), lower[...], ((1,), (0,))
        )
        moved = (trans * slope - later / (1.0 - cover)) * raw_ref[...]
        r_split = jnp.concatenate([p.astype(jnp.float32) for p in split(resid, 3)], axis=0)
        r_split = jnp.concatenate([r_split, jnp.zeros_like(resid)], axis=0).astype(jnp.bfloat16)
        d_colour = dot(r_split, w_split[0], ((1,), (0,))) + dot(r_split, w_split[1], ((1,), (0,)))
        d_colour = d_colour[0:8] + d_colour[8:16] + d_colour[16:24]
        sum0 = jnp.zeros((16, size), jnp.float32)
        sum1 = jnp.zeros((16, size), jnp.float32)
        sum2 = jnp.zeros((16, size), jnp.float32)
        for r in range(16):
            chunk = moved[16 * r : 16 * r + 16]
            first = chunk * dys[r]
            sum0 = sum0 + chunk
            sum1 = sum1 + first
            sum2 = sum2 + first * dys[r]
        m_0 = jnp.sum(sum0, axis=0, keepdims=True)
        m_x = jnp.sum(sum0 * dx, axis=0, keepdims=True)
        m_xx = jnp.sum(sum0 * dx * dx, axis=0, keepdims=True)
        m_y = jnp.sum(sum1, axis=0, keepdims=True)
        m_xy = jnp.sum(sum1 * dx, axis=0, keepdims=True)
        m_yy = jnp.sum(sum2, axis=0, keepdims=True)
        parts[me, 8 * v : 8 * v + 8, :] = jnp.concatenate(
            [
                con0 * m_x + con1 * m_y,
                con1 * m_x + con2 * m_y,
                -0.5 * m_xx,
                -m_xy,
                -0.5 * m_yy,
                d_colour[0:3],
            ],
            axis=0,
        )
        parts[me, rows + v : rows + v + 1, :] = m_0
        parts[me, rows + VIEWS + v : rows + VIEWS + v + 1, :] = square
        start, stop = 8 * v, (8 * v + 8 if v < VIEWS - 1 else rows + 8)
        for d in range(1, n_tile):
            copy = pltpu.make_async_remote_copy(
                src_ref=parts.at[me, start:stop],
                dst_ref=parts.at[me, start:stop],
                send_sem=send_g.at[v, d],
                recv_sem=recv_g.at[v, d],
                device_id={"tile": lax.rem(me + d, n_tile)},
                device_id_type=MESH,
            )
            copy.start()
            grad_sends.append(copy)

    for copy in grad_sends:
        copy.wait()
    squares = sum(parts[s, rows : rows + 8, :] for s in range(n_tile))
    totals[mg] = squares
    loss_sends = []
    for d in range(1, n_gauss):
        copy = pltpu.make_async_remote_copy(
            src_ref=totals.at[mg],
            dst_ref=totals.at[mg],
            send_sem=send_l.at[d],
            recv_sem=recv_l.at[d],
            device_id={"gauss": lax.rem(mg + d, n_gauss)},
            device_id_type=MESH,
        )
        copy.start()
        loss_sends.append(copy)

    op_block = iota((8, size), 0)
    d_views = []
    d_opacity = jnp.zeros((8, 128), jnp.float32)
    for v in range(VIEWS):
        total = jnp.zeros((8 * blocks + 8, 128), jnp.float32)
        for s in range(n_tile):
            place = id_row + v * (size // 128)
            ids = jnp.concatenate(
                [attrs[s, place + h : place + h + 1, :] for h in range(size // 128)], axis=1
            ).astype(jnp.int32)
            block, low = ids // 128 - me * blocks, ids % 128
            onehot = (low_of == low).astype(jnp.float32).astype(jnp.bfloat16)
            part = parts[s, 8 * v : 8 * v + 8, :]
            op_part = parts[s, rows + v : rows + v + 1, :]
            spread = jnp.concatenate(
                [jnp.where(block == b, part, 0.0) for b in range(blocks)]
                + [jnp.where((block == op_block) & (op_block < blocks), op_part, 0.0)],
                axis=0,
            )
            rough = spread.astype(jnp.bfloat16).astype(jnp.float32)
            both = jnp.concatenate([rough, spread - rough], axis=0).astype(jnp.bfloat16)
            added = dot(both, onehot, ((1,), (1,)))
            total = total + added[: 8 * blocks + 8] + added[8 * blocks + 8 :]
        d_views.append(
            jnp.concatenate([total[8 * b : 8 * b + 8] for b in range(blocks)], axis=1)
        )
        d_opacity = d_opacity + total[8 * blocks :]

    d_linear = []
    for v in range(VIEWS):
        value = linear_views[v]
        gate = jnp.where(value > 0.0, 1.0, jnp.where(value == 0.0, 0.5, 0.0))
        d_linear.append(jnp.where(quantity >= 5, gate * d_views[v], d_views[v]))
    grad_ref[...] = dot(table, jnp.concatenate(d_linear, axis=0), ((0,), (0,)), highest)
    g0, g1, g2 = [
        jnp.concatenate([d_views[v][2 + q : 3 + q] for v in range(VIEWS)], axis=0) for q in range(3)
    ]
    q0, q1, q2 = conic
    d_a = -(g0 * q0 * q0 + g1 * q0 * q1 + g2 * q1 * q1)
    d_b = -(2.0 * g0 * q0 * q1 + g1 * (q0 * q2 + q1 * q1) + 2.0 * g2 * q1 * q2)
    d_c = -(g0 * q1 * q1 + g1 * q1 * q2 + g2 * q2 * q2)
    d_axes = [
        [2.0 * d_a * axes[0][j] + d_b * axes[1][j] for j in range(3)],
        [2.0 * d_c * axes[1][j] + d_b * axes[0][j] for j in range(3)],
    ]
    d_mat = [
        [
            jnp.sum(
                affine[0][i] * d_axes[0][j] + affine[1][i] * d_axes[1][j], axis=0, keepdims=True
            )
            for j in range(3)
        ]
        for i in range(3)
    ]
    for j in range(3):
        grad_ref[3 + j : 4 + j, :] = stretch[j] * sum(d_mat[i][j] * rot[i][j] for i in range(3))
    d_rot = [[d_mat[i][j] * stretch[j] for j in range(3)] for i in range(3)]
    sym01, sym02, sym12 = (
        d_rot[0][1] + d_rot[1][0],
        d_rot[0][2] + d_rot[2][0],
        d_rot[1][2] + d_rot[2][1],
    )
    skew01, skew02, skew12 = (
        d_rot[1][0] - d_rot[0][1],
        d_rot[0][2] - d_rot[2][0],
        d_rot[2][1] - d_rot[1][2],
    )
    d_quat = [
        2.0 * (z * skew01 + y * skew02 + x * skew12),
        2.0 * (y * sym01 + z * sym02 - 2.0 * x * (d_rot[1][1] + d_rot[2][2]) + w * skew12),
        2.0 * (x * sym01 + z * sym12 - 2.0 * y * (d_rot[0][0] + d_rot[2][2]) + w * skew02),
        2.0 * (x * sym02 + y * sym12 - 2.0 * z * (d_rot[0][0] + d_rot[1][1]) + w * skew01),
    ]
    along = w * d_quat[0] + x * d_quat[1] + y * d_quat[2] + z * d_quat[3]
    for i, part in enumerate((w, x, y, z)):
        grad_ref[6 + i : 7 + i, :] = (d_quat[i] - part * along) / norm
    d_op = jnp.concatenate([d_opacity[b : b + 1] for b in range(blocks)], axis=1)
    grad_ref[10:11, :] = d_op * (1.0 - opacity)

    for copy in loss_sends:
        copy.wait()
    all_squares = sum(totals[g] for g in range(n_gauss))
    factor = 0.5 / (3 * 256 * n_tile * n_gauss)
    for v in range(VIEWS):
        loss_ref[v] = jnp.sum(all_squares[VIEWS + v : VIEWS + v + 1]) * factor


def shards(params, moment_one, moment_two, camera, target, tile_ids, splat_lists, counts):
    n_tile, n_gauss = lax.axis_size("tile"), lax.axis_size("gauss")
    own = params.shape[1]
    size = splat_lists.shape[2]
    blocks = own // 128
    rows = 8 * VIEWS
    id_rows = -(-(VIEWS * (size // 128)) // 8) * 8
    vmem = pl.BlockSpec(memory_space=pltpu.VMEM)
    smem = pl.BlockSpec(memory_space=pltpu.SMEM)
    dma = pltpu.SemaphoreType.DMA
    gradient, images, losses = pl.pallas_call(
        functools.partial(kernel, n_tile, n_gauss),
        out_shape=(
            jax.ShapeDtypeStruct(params.shape, jnp.float32),
            jax.ShapeDtypeStruct(target.shape, jnp.float32),
            jax.ShapeDtypeStruct((VIEWS,), jnp.float32),
        ),
        in_specs=[vmem, smem, vmem, smem, vmem, smem],
        out_specs=(vmem, vmem, smem),
        scratch_shapes=[
            pltpu.VMEM((n_tile, blocks * rows + 8 + id_rows, 128), jnp.float32),
            pltpu.VMEM((n_tile, rows + 8, size), jnp.float32),
            pltpu.VMEM((n_gauss, 8, size), jnp.float32),
            pltpu.VMEM((2 * size, size), jnp.bfloat16),
            pltpu.VMEM((2 * size, size), jnp.bfloat16),
            pltpu.VMEM((256, size), jnp.float32),
            pltpu.VMEM((256, size), jnp.float32),
            pltpu.VMEM((256, 2 * size), jnp.bfloat16),
            dma((n_tile,)),
            dma((n_tile,)),
            dma((VIEWS, n_tile)),
            dma((VIEWS, n_tile)),
            dma((n_gauss,)),
            dma((n_gauss,)),
        ],
        compiler_params=pltpu.CompilerParams(collective_id=0, has_side_effects=True),
    )(
        params,
        camera,
        target,
        tile_ids.reshape(VIEWS),
        splat_lists,
        counts.reshape(VIEWS),
    )
    rates = jnp.array(learning_rates, dtype=jnp.float32)[:, None]
    first = 0.9 * moment_one + 0.1 * gradient
    second = 0.999 * moment_two + 0.001 * gradient * gradient
    updated = params - rates * first / (jnp.sqrt(second) + 1e-15)
    return (updated, first, second, images, losses)


def solution(mesh):
    return jax.shard_map(
        shards,
        mesh=mesh,
        in_specs=(
            P(None, ("gauss", "tile")),
            P(None, ("gauss", "tile")),
            P(None, ("gauss", "tile")),
            P(),
            P(None, None, ("gauss", "tile"), None),
            P(None, ("gauss", "tile")),
            P(None, ("gauss", "tile"), None),
            P(None, ("gauss", "tile")),
        ),
        out_specs=(
            P(None, ("gauss", "tile")),
            P(None, ("gauss", "tile")),
            P(None, ("gauss", "tile")),
            P(None, None, ("gauss", "tile"), None),
            P(),
        ),
        check_vma=False,
    )
```

time: 293 us -> 37 us (0.13)
  blocking collectives: 134 us -> 0 us
  between operations: 70.3 us -> 0.67 us
  other arithmetic: 36.2 us -> 1.85 us
  Pallas kernels: 0 us -> 32.5 us
  waiting for transfers between devices: 20.6 us -> 0 us
  local copies, waits for them, and re-layouts: 21.5 us -> 1.8 us
  matrix products: 8.56 us -> 0 us
    all_gather x3 -> x0, blocking collectives: 94.5 us -> none  [shards(): band_attrs = lax.all_gather(attrs_own, 'tile', axis=1, tiled=True)]
    psum x1 -> x0, blocking collectives: 39.6 us -> none  [shards(): totals = lax.psum(jnp.stack(squared_all), ('gauss', 'tile'))]
    pallas_call x0 -> x1, Pallas kernels: none -> 32.5 us  [shards(): pl.pallas_call(functools.partial(kernel, n_tile, n_gauss), out_shape=(jax...]
    reduce_scatter x3 -> x0, waiting for transfers between devices: 20.5 us -> none  [shards(): lax.psum_scatter(band_grad, 'tile', scatter_dimension=1, tiled=True)]
    another operation x20 -> x0, other arithmetic: 12.9 us -> none
    dot_general x24 -> x0, matrix products: 8.56 us -> none  [the longest x9 5.1 us: shade(): return jnp.einsum('pj,kj->kp', weights, splat_attrs[6:9], precision=highest)]
    mul x32 -> x0, other arithmetic: 7.01 us -> none  [the longest x9 1.99 us: shade(): weights = coverage * jnp.exp(before)]
    slice x9 -> x0, local copies, waits for them, and re-layouts: 6.94 us -> none  [the longest x1 1.66 us: harmonics(): facing_x, facing_y, facing_z = (facing[0], facing[1], facing[2])]
  transfers between devices with their start and end apart: 3 -> 0, of which waited for: 1 -> 0; matrix products, arithmetic and copies ran while one was open for 12% -> 0% of each run, Pallas kernels for 0% -> 0%
where the time goes in v1:
time: 37 us; the launch traced here: 36.8 us
  Pallas kernels  32.5 us (88%)
  other arithmetic  1.85 us (5%)
  local copies, waits for them, and re-layouts  1.8 us (5%)
  between operations  0.67 us (2%)
    pallas_call x1, Pallas kernels, shards(): pl.pallas_call(functools.partial(kernel, n_tile, n_gauss), out_shape=(jax...  32.5 us
    sub x1, other arithmetic, shards(): updated = params - rates * first / (jnp.sqrt(second) + 1e-15)  1.85 us
    unnamed x10, local copies, waits for them, and re-layouts  1.8 us

profile of v1, /device:TPU:0, one launch (start us, length us, event | category | flops | bytes accessed | tf_op | source)
XLA Modules:
  0.0 36.8 jit_solution(8557368146055062662)
XLA Ops:
  0.6 0.0 copy-start
  0.6 32.5 %shard_map.128 = (f32[59,512]{1,0:T(8,128)}, f32[3,3,1,256]{3,2,1,0:T(1,128)}, f32[3]{0:T(128)}) custom-call(f32[59,512]{1,0:T(8,128)} %params_ref.1, f32[3,11]{1,0:T(4,128)} %camera.1, f32[3,3,1,256]{3,2,1,0:T(1,128)} %target_ref.1, s32[3]{0:T(128)} %bitcast.2, s32[3,1,256]{2,1,0:T(1,128)} %lists_ref.1, s32[3]{0:T(128)} %bitcast.3), custom_call_target="tpu_custom_call" | custom-call | tf_op jit(solution)/shard_map/pallas_call | solution.py:459
  33.2 0.0 copy-start.2
  33.2 0.0 copy-done
  33.2 0.6 %copy-done.2 = f32[59]{0:T(128)S(1)} copy-done((f32[59]{0:T(128)S(1)}, f32[59]{0:T(128)}, u32[]{:S(2)}) %copy-start.2) | copy-done | bytes 260
  33.8 0.0 copy-start.1
  33.8 1.8 %divide_subtract_fusion = (f32[59,512]{1,0:T(8,128)}, f32[59,512]{1,0:T(8,128)}, f32[59,512]{1,0:T(8,128)}) fusion(f32[59,512]{1,0:T(8,128)S(1)} %copy-done, f32[59]{0:T(128)S(1)} %copy-done.2, f32[59,512]{1,0:T(8,128)} %get-tuple-element.8, f32[59,512]{1,0:T(8,128)} %param.10, f32[59,512]{1,0:T(8,128)} %param.11), kind=kLoop, calls=%fused_computation.2 | loop fusion | flops 332288 | bytes 846060 | tf_op jit(solution)/shard_map/sub | solution.py:496
  35.7 0.0 copy-done.1
  35.7 0.0 copy-start.3
  35.7 0.6 %copy.16 = f32[3,3,1,256]{3,2,1,0:T(1,128)} copy(f32[3,3,1,256]{3,2,1,0:T(1,128)S(1)} %copy-done.1) | data formatting | bytes 18432
  36.3 0.0 copy-done.3
  36.3 0.5 %copy.17 = f32[3]{0:T(128)} copy(f32[3]{0:T(128)S(1)} %copy-done.3) | data formatting | bytes 24
Async XLA Ops:
  0.6 32.6 %copy-start = (f32[59,512]{1,0:T(8,128)S(1)}, f32[59,512]{1,0:T(8,128)}, u32[]{:S(2)}) copy-start(f32[59,512]{1,0:T(8,128)} %params_ref.1) | copy-start | bytes 362500
  33.2 0.7 %copy-start.2 = (f32[59]{0:T(128)S(1)}, f32[59]{0:T(128)}, u32[]{:S(2)}) copy-start(f32[59]{0:T(128)} %constant.12.clone) | copy-start | bytes 712
  33.8 1.9 %copy-start.1 = (f32[3,3,1,256]{3,2,1,0:T(1,128)S(1)}, f32[3,3,1,256]{3,2,1,0:T(1,128)}, u32[]{:S(2)}) copy-start(f32[3,3,1,256]{3,2,1,0:T(1,128)} %get-tuple-element.22) | copy-start | bytes 27652
  35.7 0.6 %copy-start.3 = (f32[3]{0:T(128)S(1)}, f32[3]{0:T(128)}, u32[]{:S(2)}) copy-start(f32[3]{0:T(128)} %get-tuple-element.23) | copy-start | bytes 40

commit v2 on v1

--- a/solution.py
+++ b/solution.py
@@ -133,7 +133,8 @@
     blocks = own // 128
     size = lists_ref.shape[2]
     rows = 8 * VIEWS
-    id_row = blocks * rows + 8
+    view_rows = 8 * blocks
+    id_row = 8 + VIEWS * view_rows
     scale = 1.0 / (VIEWS * 256)
 
     barrier = pltpu.get_barrier_semaphore()
@@ -190,14 +191,15 @@
         for q in range(3):
             value = jnp.where(quantity == 2 + q, conic[q][v : v + 1], value)
         for b in range(blocks):
-            attrs[me, b * rows + 8 * v : b * rows + 8 * v + 8, :] = value[
+            attrs[me, 8 + v * view_rows + 8 * b : 16 + v * view_rows + 8 * b, :] = value[
                 :, 128 * b : 128 * b + 128
             ]
     base = mg * (own * n_tile)
-    spare = attrs.shape[1] - blocks * rows
-    attrs[me, blocks * rows :, :] = jnp.zeros((spare, 128), jnp.float32)
+    spare = attrs.shape[1] - id_row
+    attrs[me, 0:8, :] = jnp.zeros((8, 128), jnp.float32)
+    attrs[me, id_row:, :] = jnp.zeros((spare, 128), jnp.float32)
     for b in range(blocks):
-        attrs[me, blocks * rows + b : blocks * rows + b + 1, :] = opacity[
+        attrs[me, b : b + 1, :] = opacity[
             :, 128 * b : 128 * b + 128
         ]
     for v in range(VIEWS):
@@ -208,17 +210,20 @@
 
     pl.semaphore_wait(barrier, n_tile + n_gauss - 2)
     sends = []
-    for d in range(1, n_tile):
-        copy = pltpu.make_async_remote_copy(
-            src_ref=attrs.at[me],
-            dst_ref=attrs.at[me],
-            send_sem=send_a.at[d],
-            recv_sem=recv_a.at[d],
-            device_id={"tile": lax.rem(me + d, n_tile)},
-            device_id_type=MESH,
-        )
-        copy.start()
-        sends.append(copy)
+    for v in range(VIEWS):
+        start = 8 + v * view_rows if v > 0 else 0
+        stop = 8 + (v + 1) * view_rows if v < VIEWS - 1 else attrs.shape[1]
+        for d in range(1, n_tile):
+            copy = pltpu.make_async_remote_copy(
+                src_ref=attrs.at[me, start:stop],
+                dst_ref=attrs.at[me, start:stop],
+                send_sem=send_a.at[v, d],
+                recv_sem=recv_a.at[v, d],
+                device_id={"tile": lax.rem(me + d, n_tile)},
+                device_id_type=MESH,
+            )
+            copy.start()
+            sends.append((v, copy))
 
     before_j = (iota((size, size), 0) < iota((size, size), 1)).astype(jnp.float32)
     after_j = (iota((size, size), 0) > iota((size, size), 1)).astype(jnp.float32)
@@ -226,9 +231,6 @@
         upper[c * size : (c + 1) * size, :] = before_j.astype(jnp.bfloat16)
         lower[c * size : (c + 1) * size, :] = after_j.astype(jnp.bfloat16)
     parts[me, rows + 2 * VIEWS : rows + 8, :] = jnp.zeros((8 - 2 * VIEWS, size), jnp.float32)
-    for copy in sends:
-        copy.wait()
-
     grad_sends = []
     pixel_col = iota((16, size), 0).astype(jnp.float32) + 0.5
     lane = iota((1, size), 1)
@@ -239,11 +241,12 @@
         ids = lists_ref[v] - base
         high, low = ids // 128, ids % 128
         onehot = (low_of == low).astype(jnp.float32).astype(jnp.bfloat16)
+        for view, copy in sends:
+            if view == v:
+                copy.wait()
         tiles = [
-            attrs[s, b * rows + 8 * v : b * rows + 8 * v + 8, :]
-            for s in range(n_tile)
-            for b in range(blocks)
-        ] + [attrs[s, blocks * rows : blocks * rows + 8, :] for s in range(n_tile)]
+            attrs[s, 8 + v * view_rows : 8 + (v + 1) * view_rows, :] for s in range(n_tile)
+        ] + [attrs[s, 0:8, :] for s in range(n_tile)]
         pieces = jnp.concatenate(split(jnp.concatenate(tiles, axis=0), 3), axis=1)
         picked = dot(pieces, jnp.concatenate([onehot] * 3, axis=0), ((1,), (0,)))
         splat = jnp.zeros((8, size), jnp.float32)
@@ -446,6 +449,26 @@
         loss_ref[v] = jnp.sum(all_squares[VIEWS + v : VIEWS + v + 1]) * factor
 
 
+def adam(
+    params_ref, one_ref, two_ref, grad_ref, image_ref, loss_ref, new_ref, first_ref, second_ref,
+    images_ref, losses_ref,
+):
+    row = iota(params_ref.shape, 0)
+    rates = jnp.full(params_ref.shape, learning_rates[-1], jnp.float32)
+    for i in range(len(learning_rates) - 2, -1, -1):
+        if learning_rates[i] != learning_rates[i + 1]:
+            rates = jnp.where(row <= i, learning_rates[i], rates)
+    gradient = grad_ref[...]
+    first = 0.9 * one_ref[...] + 0.1 * gradient
+    second = 0.999 * two_ref[...] + 0.001 * gradient * gradient
+    first_ref[...] = first
+    second_ref[...] = second
+    new_ref[...] = params_ref[...] - rates * first / (jnp.sqrt(second) + 1e-15)
+    images_ref[...] = image_ref[...]
+    for v in range(VIEWS):
+        losses_ref[v] = loss_ref[v]
+
+
 def shards(params, moment_one, moment_two, camera, target, tile_ids, splat_lists, counts):
     n_tile, n_gauss = lax.axis_size("tile"), lax.axis_size("gauss")
     own = params.shape[1]
@@ -474,8 +497,8 @@
             pltpu.VMEM((256, size), jnp.float32),
             pltpu.VMEM((256, size), jnp.float32),
             pltpu.VMEM((256, 2 * size), jnp.bfloat16),
-            dma((n_tile,)),
-            dma((n_tile,)),
+            dma((VIEWS, n_tile)),
+            dma((VIEWS, n_tile)),
             dma((VIEWS, n_tile)),
             dma((VIEWS, n_tile)),
             dma((n_gauss,)),
@@ -490,11 +513,14 @@
         splat_lists,
         counts.reshape(VIEWS),
     )
-    rates = jnp.array(learning_rates, dtype=jnp.float32)[:, None]
-    first = 0.9 * moment_one + 0.1 * gradient
-    second = 0.999 * moment_two + 0.001 * gradient * gradient
-    updated = params - rates * first / (jnp.sqrt(second) + 1e-15)
-    return (updated, first, second, images, losses)
+    like = jax.ShapeDtypeStruct(params.shape, jnp.float32)
+    return pl.pallas_call(
+        adam,
+        out_shape=(like, like, like, jax.ShapeDtypeStruct(target.shape, jnp.float32),
+                   jax.ShapeDtypeStruct((VIEWS,), jnp.float32)),
+        in_specs=[vmem, vmem, vmem, vmem, vmem, smem],
+        out_specs=(vmem, vmem, vmem, vmem, smem),
+    )(params, moment_one, moment_two, gradient, images, losses)
 
 
 def solution(mesh):

time: 37 us -> 33.8 us (0.914)
  other arithmetic: 1.85 us -> 0 us
  local copies, waits for them, and re-layouts: 1.8 us -> 0 us
  Pallas kernels: 32.5 us -> 33 us
    pallas_call x0 -> x1, Pallas kernels: none -> 1.91 us  [shards(): pl.pallas_call(adam, out_shape=(like, like, like, jax.ShapeDtypeStruct(ta...]
    sub x1 -> x0, other arithmetic: 1.85 us -> none  [shards(): updated = params - rates * first / (jnp.sqrt(second) + 1e-15)]
    unnamed x10 -> x0, local copies, waits for them, and re-layouts: 1.8 us -> none
    pallas_call x1, Pallas kernels: 32.5 us -> 31.1 us  [shards(): pl.pallas_call(functools.partial(kernel, n_tile, n_gauss), out_shape=(jax...]
where the time goes in v2:
time: 33.8 us; the launch traced here: 33.7 us
  Pallas kernels  33 us (98%)
  between operations  0.64 us (2%)
    pallas_call x1, Pallas kernels, shards(): pl.pallas_call(functools.partial(kernel, n_tile, n_gauss), out_shape=(jax...  31.1 us
    pallas_call x1, Pallas kernels, shards(): pl.pallas_call(adam, out_shape=(like, like, like, jax.ShapeDtypeStruct(ta...  1.91 us

profile of v2, /device:TPU:0, one launch (start us, length us, event | category | flops | bytes accessed | tf_op | source)
XLA Modules:
  0.0 33.7 jit_solution(4539246260636990563)
XLA Ops:
  0.6 31.1 %shard_map.119 = (f32[59,512]{1,0:T(8,128)}, f32[3,3,1,256]{3,2,1,0:T(1,128)}, f32[3]{0:T(128)}) custom-call(f32[59,512]{1,0:T(8,128)} %params_ref.3, f32[3,11]{1,0:T(4,128)} %camera.1, f32[3,3,1,256]{3,2,1,0:T(1,128)} %target_ref.1, s32[3]{0:T(128)} %bitcast.2, s32[3,1,256]{2,1,0:T(1,128)} %lists_ref.1, s32[3]{0:T(128)} %bitcast.3), custom_call_target="tpu_custom_call" | custom-call | tf_op jit(solution)/shard_map/pallas_call | solution.py:482
  31.7 1.9 %shard_map.120 = (f32[59,512]{1,0:T(8,128)}, f32[59,512]{1,0:T(8,128)}, f32[59,512]{1,0:T(8,128)}, f32[3,3,1,256]{3,2,1,0:T(1,128)}, f32[3]{0:T(128)}) custom-call(f32[59,512]{1,0:T(8,128)} %params_ref.3, f32[59,512]{1,0:T(8,128)} %one_ref.1, f32[59,512]{1,0:T(8,128)} %two_ref.1, f32[59,512]{1,0:T(8,128)} %get-tuple-element.8.grad_ref, ...), custom_call_target="tpu_custom_call" | custom-call | tf_op jit(solution)/shard_map/pallas_call | solution.py:517

commit v3 on v2

--- a/solution.py
+++ b/solution.py
@@ -101,21 +101,34 @@
     return out
 
 
+def part_rows(view):
+    if view < VIEWS - 1:
+        return 8 * view, 8 * (VIEWS - 1) + view
+    return 8 * VIEWS, 8 * VIEWS + 8
+
+
 def kernel(
     n_tile,
     n_gauss,
+    params_hbm,
+    camera_hbm,
+    target_hbm,
+    tiles_hbm,
+    lists_hbm,
+    counts_hbm,
+    grad_ref,
+    image_ref,
+    loss_ref,
     params_ref,
     camera,
     target_ref,
     tile_ids,
     lists_ref,
     counts,
-    grad_ref,
-    image_ref,
-    loss_ref,
     attrs,
     parts,
     totals,
+    sums,
     upper,
     lower,
     alpha_ref,
@@ -127,6 +140,9 @@
     recv_g,
     send_l,
     recv_l,
+    send_s,
+    recv_s,
+    load_sem,
 ):
     me, mg = lax.axis_index("tile"), lax.axis_index("gauss")
     n_params, own = params_ref.shape
@@ -136,6 +152,7 @@
     view_rows = 8 * blocks
     id_row = 8 + VIEWS * view_rows
     scale = 1.0 / (VIEWS * 256)
+    near_first = sorted(range(1, n_tile), key=lambda d: (min(d, n_tile - d), d))
 
     barrier = pltpu.get_barrier_semaphore()
     for d in range(1, n_tile):
@@ -146,6 +163,23 @@
         pl.semaphore_signal(
             barrier, inc=1, device_id={"gauss": lax.rem(mg + d, n_gauss)}, device_id_type=MESH
         )
+
+    loads = []
+    for i, (source, target) in enumerate(
+        (
+            (camera_hbm, camera),
+            (params_hbm, params_ref),
+            (lists_hbm, lists_ref),
+            (counts_hbm, counts),
+            (tiles_hbm, tile_ids),
+            (target_hbm, target_ref),
+        )
+    ):
+        copy = pltpu.make_async_copy(source, target, load_sem.at[i])
+        copy.start()
+        loads.append(copy)
+    for copy in loads:
+        copy.wait()
 
     table = basis(camera, n_params)
     view_of = iota((VIEWS, own), 0)
@@ -213,7 +247,7 @@
     for v in range(VIEWS):
         start = 8 + v * view_rows if v > 0 else 0
         stop = 8 + (v + 1) * view_rows if v < VIEWS - 1 else attrs.shape[1]
-        for d in range(1, n_tile):
+        for d in near_first:
             copy = pltpu.make_async_remote_copy(
                 src_ref=attrs.at[me, start:stop],
                 dst_ref=attrs.at[me, start:stop],
@@ -230,8 +264,8 @@
     for c in range(2):
         upper[c * size : (c + 1) * size, :] = before_j.astype(jnp.bfloat16)
         lower[c * size : (c + 1) * size, :] = after_j.astype(jnp.bfloat16)
-    parts[me, rows + 2 * VIEWS : rows + 8, :] = jnp.zeros((8 - 2 * VIEWS, size), jnp.float32)
-    grad_sends = []
+    parts[me, 8 * VIEWS - 8 : 8 * VIEWS, :] = jnp.zeros((8, size), jnp.float32)
+    grad_sends, loss_sends, squares = [], [], []
     pixel_col = iota((16, size), 0).astype(jnp.float32) + 0.5
     lane = iota((1, size), 1)
     low_of = iota((128, size), 0)
@@ -294,6 +328,22 @@
             residual = image[k : k + 1] - target_ref[v, k]
             square = square + residual * residual
             residuals.append(residual * scale)
+        squares.append(square[:, 0:128] + square[:, 128:256])
+        if v == VIEWS - 1:
+            totals[mg] = jnp.concatenate(
+                squares + [jnp.zeros((8 - VIEWS, 128), jnp.float32)], axis=0
+            )
+            for d in range(1, n_gauss):
+                copy = pltpu.make_async_remote_copy(
+                    src_ref=totals.at[mg],
+                    dst_ref=totals.at[mg],
+                    send_sem=send_l.at[d],
+                    recv_sem=recv_l.at[d],
+                    device_id={"gauss": lax.rem(mg + d, n_gauss)},
+                    device_id_type=MESH,
+                )
+                copy.start()
+                loss_sends.append(copy)
         resid = jnp.concatenate(residuals + [jnp.zeros((5, 256), jnp.float32)], axis=0)
         slope = dot(resid, colour, ((0,), (0,)), highest)
         later = dot(
@@ -319,7 +369,8 @@
         m_y = jnp.sum(sum1, axis=0, keepdims=True)
         m_xy = jnp.sum(sum1 * dx, axis=0, keepdims=True)
         m_yy = jnp.sum(sum2, axis=0, keepdims=True)
-        parts[me, 8 * v : 8 * v + 8, :] = jnp.concatenate(
+        first_row, op_place = part_rows(v)
+        parts[me, first_row : first_row + 8, :] = jnp.concatenate(
             [
                 con0 * m_x + con1 * m_y,
                 con1 * m_x + con2 * m_y,
@@ -330,10 +381,10 @@
             ],
             axis=0,
         )
-        parts[me, rows + v : rows + v + 1, :] = m_0
-        parts[me, rows + VIEWS + v : rows + VIEWS + v + 1, :] = square
-        start, stop = 8 * v, (8 * v + 8 if v < VIEWS - 1 else rows + 8)
-        for d in range(1, n_tile):
+        parts[me, op_place : op_place + 1, :] = m_0
+        start = first_row
+        stop = first_row + (8 if v < VIEWS - 2 else 16 if v == VIEWS - 2 else 9)
+        for d in near_first:
             copy = pltpu.make_async_remote_copy(
                 src_ref=parts.at[me, start:stop],
                 dst_ref=parts.at[me, start:stop],
@@ -343,29 +394,34 @@
                 device_id_type=MESH,
             )
             copy.start()
-            grad_sends.append(copy)
-
-    for copy in grad_sends:
-        copy.wait()
-    squares = sum(parts[s, rows : rows + 8, :] for s in range(n_tile))
-    totals[mg] = squares
-    loss_sends = []
-    for d in range(1, n_gauss):
-        copy = pltpu.make_async_remote_copy(
-            src_ref=totals.at[mg],
-            dst_ref=totals.at[mg],
-            send_sem=send_l.at[d],
-            recv_sem=recv_l.at[d],
-            device_id={"gauss": lax.rem(mg + d, n_gauss)},
-            device_id_type=MESH,
-        )
-        copy.start()
-        loss_sends.append(copy)
+            grad_sends.append((v, copy))
 
     op_block = iota((8, size), 0)
     d_views = []
     d_opacity = jnp.zeros((8, 128), jnp.float32)
     for v in range(VIEWS):
+        if v == VIEWS - 1:
+            for copy in loss_sends:
+                copy.wait()
+            loss_sends = []
+            sums[me] = sum(totals[g] for g in range(n_gauss))
+            for d in range(1, n_tile):
+                copy = pltpu.make_async_remote_copy(
+                    src_ref=sums.at[me],
+                    dst_ref=sums.at[me],
+                    send_sem=send_s.at[d],
+                    recv_sem=recv_s.at[d],
+                    device_id={"tile": lax.rem(me + d, n_tile)},
+                    device_id_type=MESH,
+                )
+                copy.start()
+                loss_sends.append(copy)
+        ready = max(v, VIEWS - 2)
+        for view, copy in grad_sends:
+            if view <= ready:
+                copy.wait()
+        grad_sends = [pair for pair in grad_sends if pair[0] > ready]
+        first_row, op_place = part_rows(v)
         total = jnp.zeros((8 * blocks + 8, 128), jnp.float32)
         for s in range(n_tile):
             place = id_row + v * (size // 128)
@@ -374,8 +430,8 @@
             ).astype(jnp.int32)
             block, low = ids // 128 - me * blocks, ids % 128
             onehot = (low_of == low).astype(jnp.float32).astype(jnp.bfloat16)
-            part = parts[s, 8 * v : 8 * v + 8, :]
-            op_part = parts[s, rows + v : rows + v + 1, :]
+            part = parts[s, first_row : first_row + 8, :]
+            op_part = parts[s, op_place : op_place + 1, :]
             spread = jnp.concatenate(
                 [jnp.where(block == b, part, 0.0) for b in range(blocks)]
                 + [jnp.where((block == op_block) & (op_block < blocks), op_part, 0.0)],
@@ -443,10 +499,10 @@
 
     for copy in loss_sends:
         copy.wait()
-    all_squares = sum(totals[g] for g in range(n_gauss))
+    all_squares = sum(sums[s] for s in range(n_tile))
     factor = 0.5 / (3 * 256 * n_tile * n_gauss)
     for v in range(VIEWS):
-        loss_ref[v] = jnp.sum(all_squares[VIEWS + v : VIEWS + v + 1]) * factor
+        loss_ref[v] = jnp.sum(all_squares[v : v + 1]) * factor
 
 
 def adam(
@@ -486,12 +542,19 @@
             jax.ShapeDtypeStruct(target.shape, jnp.float32),
             jax.ShapeDtypeStruct((VIEWS,), jnp.float32),
         ),
-        in_specs=[vmem, smem, vmem, smem, vmem, smem],
+        in_specs=[pl.BlockSpec(memory_space=pltpu.HBM)] * 6,
         out_specs=(vmem, vmem, smem),
         scratch_shapes=[
+            pltpu.VMEM(params.shape, jnp.float32),
+            pltpu.SMEM(camera.shape, jnp.float32),
+            pltpu.VMEM(target.shape, jnp.float32),
+            pltpu.SMEM((VIEWS,), jnp.int32),
+            pltpu.VMEM(splat_lists.shape, jnp.int32),
+            pltpu.SMEM((VIEWS,), jnp.int32),
             pltpu.VMEM((n_tile, blocks * rows + 8 + id_rows, 128), jnp.float32),
-            pltpu.VMEM((n_tile, rows + 8, size), jnp.float32),
-            pltpu.VMEM((n_gauss, 8, size), jnp.float32),
+            pltpu.VMEM((n_tile, rows + 9, size), jnp.float32),
+            pltpu.VMEM((n_gauss, 8, 128), jnp.float32),
+            pltpu.VMEM((n_tile, 8, 128), jnp.float32),
             pltpu.VMEM((2 * size, size), jnp.bfloat16),
             pltpu.VMEM((2 * size, size), jnp.bfloat16),
             pltpu.VMEM((256, size), jnp.float32),
@@ -503,6 +566,9 @@
             dma((VIEWS, n_tile)),
             dma((n_gauss,)),
             dma((n_gauss,)),
+            dma((n_tile,)),
+            dma((n_tile,)),
+            dma((6,)),
         ],
         compiler_params=pltpu.CompilerParams(collective_id=0, has_side_effects=True),
     )(

time: 33.8 us -> 32.8 us (0.970)
  Pallas kernels: 33 us -> 32 us
    pallas_call x1, Pallas kernels: 31.1 us -> 30 us  [shards(): pl.pallas_call(functools.partial(kernel, n_tile, n_gauss), out_shape=(jax...]
where the time goes in v3:
time: 32.8 us; the launch traced here: 32.6 us
  Pallas kernels  32 us (98%)
  between operations  0.64 us (2%)
    pallas_call x1, Pallas kernels, shards(): pl.pallas_call(functools.partial(kernel, n_tile, n_gauss), out_shape=(jax...  30 us
    pallas_call x1, Pallas kernels, shards(): pl.pallas_call(adam, out_shape=(like, like, like, jax.ShapeDtypeStruct(ta...  1.91 us

profile of v3, /device:TPU:0, one launch (start us, length us, event | category | flops | bytes accessed | tf_op | source)
XLA Modules:
  0.0 32.6 jit_solution(4721979278606273196)
XLA Ops:
  0.6 30.0 %shard_map.119 = (f32[59,512]{1,0:T(8,128)}, f32[3,3,1,256]{3,2,1,0:T(1,128)}, f32[3]{0:T(128)}) custom-call(f32[59,512]{1,0:T(8,128)} %params_ref.1, f32[3,11]{1,0:T(4,128)} %camera_hbm.1, f32[3,3,1,256]{3,2,1,0:T(1,128)} %target_hbm.1, s32[3]{0:T(128)} %bitcast.2, s32[3,1,256]{2,1,0:T(1,128)} %lists_hbm.1, s32[3]{0:T(128)} %bitcast.3), custom_call_target="tpu_custom_call" | custom-call | tf_op jit(solution)/shard_map/pallas_call | solution.py:538
  30.7 1.9 %shard_map.120 = (f32[59,512]{1,0:T(8,128)}, f32[59,512]{1,0:T(8,128)}, f32[59,512]{1,0:T(8,128)}, f32[3,3,1,256]{3,2,1,0:T(1,128)}, f32[3]{0:T(128)}) custom-call(f32[59,512]{1,0:T(8,128)} %params_ref.1, f32[59,512]{1,0:T(8,128)} %one_ref.1, f32[59,512]{1,0:T(8,128)} %two_ref.1, f32[59,512]{1,0:T(8,128)} %get-tuple-element.8.grad_ref, ...), custom_call_target="tpu_custom_call" | custom-call | tf_op jit(solution)/shard_map/pallas_call | solution.py:583
